TPU v7x, 256 devices: a whole 4x4x8 slice. The times are simulated.
256 devices in a mesh: dp: 32 (over x, z), ctx: 8 (over y, core).
Axes of the slice: x: 4, y: 4, z: 8, core: 2. Of those that a mesh axis runs over, the one named last changes fastest.
Arguments:
- layer_input: bfloat16 [32, 1024, 4096], P('dp', 'ctx'), may hold values from -6 to 6
- queries: bfloat16 [32, 1024, 4096], P('dp', 'ctx'), may hold values from -4.5 to 4.5
- keys_saved: bfloat16 [32, 1024, 1024], P('dp', 'ctx'), may hold values from -4.5 to 4.5
- values_saved: bfloat16 [32, 1024, 1024], P('dp', 'ctx'), may hold values from -6 to 6
- out_grad: bfloat16 [32, 1024, 4096], P('dp', 'ctx'), may hold values from -6 to 6
- master_weight: float32 [4096, 6144], P('dp', 'ctx'), may hold values from -2 to 2
- first_moment: float32 [4096, 6144], P('dp', 'ctx'), may hold values from -100 to 100
- second_moment: float32 [4096, 6144], P('dp', 'ctx'), may hold values from 10 to 3000
Outputs:
- first_new: float32 [4096, 6144], P('dp', 'ctx')
- second_new: float32 [4096, 6144], P('dp', 'ctx')
- lamb_update: float32 [4096, 6144], P('dp', 'ctx')
- new_weights: bfloat16 [4096, 6144], P(None, 'ctx')
All inputs are finite; a program needn't handle non-finite values.
Results may differ from a plain program's by a relative error of at most 0.0095.
Values may be sent and summed in bfloat16 or wider, within the bound.
No kernel may reach another device: no remote copies, remote signals or barrier semaphores. Data moves between devices by JAX's collectives and lax.ppermute only.
A program may use at most 128 MiB of HBM per device.

v0:
```python
import jax
import jax.numpy as jnp
from jax import lax
from jax.sharding import PartitionSpec as P

HEAD_DIM = 128
STEP = 100
beta_first = 0.9
beta_second = 0.999
adam_epsilon = 1e-06
decay_rate = 0.01
learn_rate = 0.01
masked_score = -1e30


def head_grads(query_local, key_local, value_local, grad_local):
    length = query_local.shape[0]
    kv_local = key_local.shape[1] // HEAD_DIM
    group_size = query_local.shape[1] // key_local.shape[1]
    block_rows = min(512, length)
    block_count = length // block_rows
    score_scale = HEAD_DIM ** (-0.5)
    query_blocks = query_local.reshape(block_count, block_rows, kv_local, group_size, HEAD_DIM)
    grad_blocks = grad_local.reshape(block_count, block_rows, kv_local, group_size, HEAD_DIM)
    key_rows = key_local.reshape(length, kv_local, HEAD_DIM)
    value_rows = value_local.reshape(length, kv_local, HEAD_DIM)
    positions = jnp.arange(length)

    def one_block(accums, block_items):
        key_acc, value_acc = accums
        query_blk, grad_blk, block_start = block_items
        scores = (
            jnp.einsum("qgrd,kgd->grqk", query_blk, key_rows, preferred_element_type=jnp.float32)
            * score_scale
        )
        query_pos = block_start + jnp.arange(block_rows)
        allowed = positions[None, :] <= query_pos[:, None]
        scores = jnp.where(allowed, scores, masked_score)
        row_max = jnp.max(scores, axis=-1, keepdims=True)
        weights = jnp.exp(scores - row_max)
        probabilities = weights / jnp.sum(weights, axis=-1, keepdims=True)
        probs_b = probabilities.astype(jnp.bfloat16)
        attended = jnp.einsum(
            "grqk,kgd->qgrd", probs_b, value_rows, preferred_element_type=jnp.float32
        )
        row_delta = jnp.sum(grad_blk.astype(jnp.float32) * attended, axis=-1)
        prob_grad = jnp.einsum(
            "qgrd,kgd->grqk", grad_blk, value_rows, preferred_element_type=jnp.float32
        )
        dscore = (
            probabilities * (prob_grad - jnp.transpose(row_delta, (1, 2, 0))[..., None])
        ).astype(jnp.bfloat16)
        query_grad = (
            jnp.einsum("grqk,kgd->qgrd", dscore, key_rows, preferred_element_type=jnp.float32)
            * score_scale
        ).astype(jnp.bfloat16)
        key_acc = key_acc + jnp.einsum(
            "grqk,qgrd->kgd", dscore, query_blk, preferred_element_type=jnp.float32
        )
        value_acc = value_acc + jnp.einsum(
            "grqk,qgrd->kgd", probs_b, grad_blk, preferred_element_type=jnp.float32
        )
        return ((key_acc, value_acc), query_grad)

    starts = jnp.arange(block_count) * block_rows
    empty_acc = jnp.zeros((length, kv_local, HEAD_DIM), jnp.float32)
    (key_acc, value_acc), query_grads = lax.scan(
        one_block, (empty_acc, empty_acc), (query_blocks, grad_blocks, starts)
    )
    query_grad = query_grads.reshape(length, kv_local, group_size * HEAD_DIM)
    key_grad = (key_acc * score_scale).astype(jnp.bfloat16)
    value_grad = value_acc.astype(jnp.bfloat16)
    return jnp.concatenate([query_grad, key_grad, value_grad], axis=2).reshape(length, -1)


def body(
    layer_input,
    queries,
    keys_saved,
    values_saved,
    out_grad,
    master_weight,
    first_moment,
    second_moment,
):
    weight_sq = jnp.sum(master_weight * master_weight)
    query_heads, key_heads, value_heads, grad_heads = (
        lax.all_to_all(queries, "ctx", split_axis=2, concat_axis=1, tiled=True),
        lax.all_to_all(keys_saved, "ctx", split_axis=2, concat_axis=1, tiled=True),
        lax.all_to_all(values_saved, "ctx", split_axis=2, concat_axis=1, tiled=True),
        lax.all_to_all(out_grad, "ctx", split_axis=2, concat_axis=1, tiled=True),
    )
    grouped = head_grads(query_heads[0], key_heads[0], value_heads[0], grad_heads[0])
    partial_value = lax.dot_general(
        lax.all_gather(layer_input, "ctx", axis=1, tiled=True)[0],
        grouped,
        (((0,), (0,)), ((), ())),
        preferred_element_type=jnp.float32,
    )
    gradient = lax.psum_scatter(
        partial_value.astype(jnp.bfloat16), "dp", scatter_dimension=0, tiled=True
    ).astype(jnp.float32)
    first_new = beta_first * first_moment + (1.0 - beta_first) * gradient
    second_new = beta_second * second_moment + (1.0 - beta_second) * gradient * gradient
    corr_first = 1.0 - beta_first**STEP
    corr_second = 1.0 - beta_second**STEP
    direction = (
        first_new / corr_first / (jnp.sqrt(second_new / corr_second) + adam_epsilon)
        + decay_rate * master_weight
    )
    update_sq = jnp.sum(direction * direction)
    weight_total, update_total = lax.psum((weight_sq, update_sq), ("dp", "ctx"))
    trust_ratio = jnp.sqrt(weight_total) / jnp.sqrt(update_total)
    lamb_update = trust_ratio * direction
    new_local = (master_weight - learn_rate * lamb_update).astype(jnp.bfloat16)
    new_weights = lax.all_gather(new_local, "dp", axis=0, tiled=True)
    return (first_new, second_new, lamb_update, new_weights)


def solution(mesh):
    in_specs = (
        P("dp", "ctx", None),
        P("dp", "ctx", None),
        P("dp", "ctx", None),
        P("dp", "ctx", None),
        P("dp", "ctx", None),
        P("dp", "ctx"),
        P("dp", "ctx"),
        P("dp", "ctx"),
    )
    out_specs = (P("dp", "ctx"), P("dp", "ctx"), P("dp", "ctx"), P(None, "ctx"))
    return jax.shard_map(body, mesh=mesh, in_specs=in_specs, out_specs=out_specs, check_vma=False)
```

profile of v0, /device:TPU:36, one launch (start us, length us, event | category | flops | bytes accessed | tf_op | source)
XLA Modules:
  0.0 623.9 jit_solution(10160004014047542531)
XLA Ops:
  11.9 4.5 all-to-all-start.3
  23.9 4.0 all-to-all-start.1
  28.0 5.0 copy.102
  33.0 22.4 %reduce.3 = bf16[4096,128]{1,0:T(8,128)(2,1)S(1)} reduce(bf16[4096,1,128]{2,1,0:T(2,128)(2,1)S(1)} %bitcast.220, bf16[]{:T(256)} %broadcast.70), dimensions={1}, to_apply=%bitcast.150.reduce_sub_computation | reduce | bytes 2097154
  56.6 4.7 all-to-all-start
  61.2 5.0 copy.106
  66.3 23.4 %reduce.5 = bf16[4096,128]{1,0:T(8,128)(2,1)} reduce(bf16[4096,1,128]{2,1,0:T(2,128)(2,1)S(1)} %bitcast.219, bf16[]{:T(256)} %broadcast.70), dimensions={1}, to_apply=%bitcast.154.reduce_sub_computation | reduce | bytes 2097154
  91.9 4.8 all-to-all-start.2
  100.3 4.3 reshape.108
  107.5 5.3 all-to-all-done.2
  112.7 5.9 reshape.112
  123.8 66.4 %while.15 = (s32[]{:T(128)}, f32[1024,1,128]{0,2,1:T(8,128)S(1)}, f32[1024,1,128]{0,2,1:T(8,128)}, bf16[2,512,1,4,128]{4,3,1,0,2:T(4,128)(2,1)}, bf16[2,512,1,4,...) while((s32[]{:T(128)}, f32[1024,1,128]{0,2,1:T(8,128)S(1)}, ...), condition=%wide.region_4.5_spmd.clone, body=%wide.region_0.4_spmd.clone.sunk | while | flops 3273910784 | bytes 178353008 | solution.py:67
  134.9 5.3 fusion.84
  141.1 3.5 fusion.85
  149.1 7.3 %fusion.87 = f32[1024,1,128]{0,2,1:T(8,128)} fusion(bf16[1,512,1,4,128]{4,3,1,0,2:T(4,128)(2,1)S(1)} %get-tuple-element.238, f32[1024,1,128]{0,2,1:T(8,128)} %get-tuple-element.255, pred[]{:T(512)S(6)} %compare.3, f32[4,512]{1,0:T(4,128)S(1)} %fusion.83, f32[4,512]{1,0:T(4,128)S(1)} %get-tuple-element.241, f32[512,4,1024]{2,0,1:T(8,128)} %copy-done, ...), kind=kOutput, calls=%fused_computation.23.clone.1 | convolution fusion | flops 547618816 | bytes 10502145 | tf_op jit(solution)/shard_map/while/body/eval_jaxpr/grqk,qgrd->kgd/dot_general | solution.py:60
  168.3 5.3 fusion.84
  174.2 3.5 fusion.85
  182.2 7.2 %fusion.87 = f32[1024,1,128]{0,2,1:T(8,128)} fusion(bf16[1,512,1,4,128]{4,3,1,0,2:T(4,128)(2,1)S(1)} %get-tuple-element.238, f32[1024,1,128]{0,2,1:T(8,128)} %get-tuple-element.255, pred[]{:T(512)S(6)} %compare.3, f32[4,512]{1,0:T(4,128)S(1)} %fusion.83, f32[4,512]{1,0:T(4,128)S(1)} %get-tuple-element.241, f32[512,4,1024]{2,0,1:T(8,128)} %copy-done, ...), kind=kOutput, calls=%fused_computation.23.clone.1 | convolution fusion | flops 547618816 | bytes 10502145 | tf_op jit(solution)/shard_map/while/body/eval_jaxpr/grqk,qgrd->kgd/dot_general | solution.py:60
  193.5 12.3 %fusion.45 = bf16[4096,768]{0,1:T(8,128)(2,1)} fusion(bf16[1,1024,4096]{2,1,0:T(8,128)(2,1)} %all-gather.3.cloned.1.call-done, bf16[1024,1,128]{2,0,1:T(8,128)(2,1)S(1)} %copy.115, bf16[1024,1,128]{2,0,1:T(8,128)(2,1)S(1)} %multiply_convert_fusion, bf16[1024,1,512]{2,0,1:T(8,128)(2,1)S(1)} %reshape.90), kind=kOutput, calls=%fused_computation.42 | convolution fusion | flops 6450315264 | bytes 16252928 | tf_op jit(solution)/shard_map/dot_general | solution.py:94
  205.8 8.7 %copy.129 = bf16[4096,768]{1,0:T(8,128)(2,1)} copy(bf16[4096,768]{0,1:T(8,128)(2,1)} %fusion.45) | data formatting | bytes 12582912
  215.8 222.4 %reduce-scatter.4.cloned.1.call-done = bf16[128,768]{1,0:T(8,128)(2,1)} async-done(((bf16[4096,768]{1,0:T(8,128)(2,1)}), bf16[128,768]{1,0:T(8,128)(2,1)}) %reduce-scatter.4.cloned.1.call-update) | async-done | bytes 196624
  440.2 74.4 %all-reduce = (f32[]{:T(128)}, f32[]{:T(128)}) all-reduce(f32[]{:T(128)} %multiply_reduce_fusion.1, f32[]{:T(128)} %get-tuple-element.171), channel_id=1, replica_groups=mesh['dp'=32,'ctx'=8] {'dp','ctx'}, use_global_device_ids=true, to_apply=%region_7.8 | all-reduce | flops 2 | bytes 16 | tf_op jit(solution)/shard_map/psum | solution.py:112
  519.6 89.2 %all-gather.5.cloned.1.call-done = bf16[4096,768]{0,1:T(8,128)(2,1)} async-done(((bf16[128,768]{0,1:T(8,128)(2,1)}), bf16[4096,768]{0,1:T(8,128)(2,1)}) %all-gather.5.cloned.1.call-update) | async-done | bytes 6291472 | tf_op jit(solution)/shard_map/all_gather | solution.py:116
  608.8 8.6 %copy.122 = bf16[4096,768]{1,0:T(8,128)(2,1)} copy(bf16[4096,768]{0,1:T(8,128)(2,1)} %all-gather.5.cloned.1.call-done) | data formatting | bytes 12582912
  (106 shorter events, 71.2 us)
Async XLA Ops:
  11.9 12.0 %all-to-all-start.3 = ((bf16[8,2,8192]{2,1,0:T(2,128)(2,1)}), bf16[8,2,8192]{2,1,0:T(2,128)(2,1)S(1)}, u32[]{:S(2)}, u32[]{:S(2)}) async-start(bf16[8,2,8192]{2,1,0:T(2,128)(2,1)} %reshape.113), calls=%async_computation.3 | async-start | bytes 524288 | tf_op jit(solution)/shard_map/all_to_all | solution.py:90
  23.9 32.6 %all-to-all-start.1 = ((bf16[8,2,8192]{2,1,0:T(2,128)(2,1)}), bf16[8,2,8192]{2,1,0:T(2,128)(2,1)}, u32[]{:S(2)}, u32[]{:S(2)}) async-start(bf16[8,2,8192]{2,1,0:T(2,128)(2,1)} %reshape.109), calls=%async_computation.1 | async-start | bytes 524288 | tf_op jit(solution)/shard_map/all_to_all | solution.py:89
  56.6 35.3 %all-to-all-start = ((bf16[8,2,32768]{2,1,0:T(2,128)(2,1)}), bf16[8,2,32768]{2,1,0:T(2,128)(2,1)S(1)}, u32[]{:S(2)}, u32[]{:S(2)}) async-start(bf16[8,2,32768]{2,1,0:T(2,128)(2,1)} %reshape.107), calls=%async_computation | async-start | bytes 2097152 | tf_op jit(solution)/shard_map/all_to_all | solution.py:88
  91.9 8.2 %copy-start.6 = (bf16[8,2,32768]{2,1,0:T(2,128)(2,1)}, bf16[8,2,32768]{2,1,0:T(2,128)(2,1)S(1)}, u32[]{:S(2)}) copy-start(bf16[8,2,32768]{2,1,0:T(2,128)(2,1)S(1)} %all-to-all-done) | copy-start | bytes 3145732
  91.9 20.9 %all-to-all-start.2 = ((bf16[8,2,32768]{2,1,0:T(2,128)(2,1)}), bf16[8,2,32768]{2,1,0:T(2,128)(2,1)}, u32[]{:S(2)}, u32[]{:S(2)}) async-start(bf16[8,2,32768]{2,1,0:T(2,128)(2,1)} %reshape.111), calls=%async_computation.2 | async-start | bytes 2097152 | tf_op jit(solution)/shard_map/all_to_all | solution.py:91
  96.7 96.8 %all-gather.3.cloned.1.call-start = ((), (), s32[]{:S(2)}) async-start(), calls=%async_computation.5 | async-start | bytes 9437184 | tf_op jit(solution)/shard_map/all_gather | solution.py:95
  97.4 340.8 %reduce-scatter.4.cloned.1.call-start = ((), (), s32[]{:S(2)}) async-start(), calls=%async_computation.7 | async-start | bytes 6488064
  123.8 10.7 %copy-start.4 = (bf16[2,512,1,4,128]{4,3,1,0,2:T(4,128)(2,1)}, bf16[2,512,1,4,128]{4,3,1,0,2:T(4,128)(2,1)S(1)}, u32[]{:S(2)}) copy-start(bf16[2,512,1,4,128]{4,3,1,0,2:T(4,128)(2,1)S(1)} %get-tuple-element.268) | copy-start | bytes 3145732 | tf_op jit(solution)/shard_map/while
  128.8 3.2 copy-start
  134.8 6.2 %copy-start.1 = (f32[512,4,1024]{2,0,1:T(8,128)S(1)}, f32[512,4,1024]{2,0,1:T(8,128)}, u32[]{:S(2)}) copy-start(f32[512,4,1024]{2,0,1:T(8,128)} %copy-done) | copy-start | bytes 25165828 | tf_op jit(solution)/shard_map/while
  134.8 6.2 copy-start.10
  144.6 2.0 copy-start.2
  149.1 7.3 %copy-start.3 = (bf16[4,512,1024]{2,1,0:T(8,128)(2,1)S(1)}, bf16[4,512,1024]{2,1,0:T(8,128)(2,1)}, u32[]{:S(2)}) copy-start(bf16[4,512,1024]{2,1,0:T(8,128)(2,1)} %copy-done.2) | copy-start | bytes 12582916 | tf_op jit(solution)/shard_map/while
  149.1 8.1 %copy-start.5 = (bf16[2,512,1,4,128]{4,3,1,0,2:T(4,128)(2,1)S(1)}, bf16[2,512,1,4,128]{4,3,1,0,2:T(4,128)(2,1)}, u32[]{:S(2)}) copy-start(bf16[2,512,1,4,128]{4,3,1,0,2:T(4,128)(2,1)} %copy-done.4) | copy-start | bytes 3145732 | tf_op jit(solution)/shard_map/while
  157.2 10.7 %copy-start.4 = (bf16[2,512,1,4,128]{4,3,1,0,2:T(4,128)(2,1)}, bf16[2,512,1,4,128]{4,3,1,0,2:T(4,128)(2,1)S(1)}, u32[]{:S(2)}) copy-start(bf16[2,512,1,4,128]{4,3,1,0,2:T(4,128)(2,1)S(1)} %get-tuple-element.268) | copy-start | bytes 3145732 | tf_op jit(solution)/shard_map/while
  162.2 3.2 copy-start
  168.2 5.9 copy-start.1
  168.2 5.9 copy-start.10
  182.2 7.3 %copy-start.3 = (bf16[4,512,1024]{2,1,0:T(8,128)(2,1)S(1)}, bf16[4,512,1024]{2,1,0:T(8,128)(2,1)}, u32[]{:S(2)}) copy-start(bf16[4,512,1024]{2,1,0:T(8,128)(2,1)} %copy-done.2) | copy-start | bytes 12582916 | tf_op jit(solution)/shard_map/while
  182.2 8.1 %copy-start.5 = (bf16[2,512,1,4,128]{4,3,1,0,2:T(4,128)(2,1)S(1)}, bf16[2,512,1,4,128]{4,3,1,0,2:T(4,128)(2,1)}, u32[]{:S(2)}) copy-start(bf16[2,512,1,4,128]{4,3,1,0,2:T(4,128)(2,1)} %copy-done.4) | copy-start | bytes 3145732 | tf_op jit(solution)/shard_map/while
  205.7 8.8 %copy-start.7 = (f32[128,768]{1,0:T(8,128)S(1)}, f32[128,768]{1,0:T(8,128)}, u32[]{:S(2)}) copy-start(f32[128,768]{1,0:T(8,128)} %param.15) | copy-start | bytes 1179652
  205.7 9.0 %copy-start.8 = (f32[128,768]{1,0:T(8,128)S(1)}, f32[128,768]{1,0:T(8,128)}, u32[]{:S(2)}) copy-start(f32[128,768]{1,0:T(8,128)} %param.16) | copy-start | bytes 1179652
  205.7 9.2 %copy-start.9 = (f32[128,768]{1,0:T(8,128)S(1)}, f32[128,768]{1,0:T(8,128)}, u32[]{:S(2)}) copy-start(f32[128,768]{1,0:T(8,128)} %param.17) | copy-start | bytes 1179652
  214.5 394.2 %all-gather.5.cloned.1.call-start = ((), (), s32[]{:S(2)}) async-start(), calls=%async_computation.6 | async-start | bytes 6488064 | tf_op jit(solution)/shard_map/all_gather | solution.py:116
  (1 other events, 2.0 us)
Sparse Core Ops, SparseCore 0:
  99.4 55.1 all-gather.2
  214.6 223.5 reduce-scatter.3
  516.9 91.7 all-gather.4
where the time goes:
time: 626 us; the launch traced here: 624 us
  waiting for transfers between devices  321 us (51%)
  local copies, waits for them, and re-layouts  83 us (13%)
  blocking collectives  74.4 us (12%)
  other arithmetic  59.6 us (10%)
  matrix products  52.3 us (8%)
  starting transfers between devices  18.1 us (3%)
  between operations  15.4 us (2%)
    unnamed x4, waiting for transfers between devices  223 us
    all_gather x1, waiting for transfers between devices, body(): new_weights = lax.all_gather(new_local, 'dp', axis=0, tiled=True)  89.2 us
    psum x1, blocking collectives, body(): weight_total, update_total = lax.psum((weight_sq, update_sq), ('dp', 'ctx'))  74.4 us
    unnamed x35, local copies, waits for them, and re-layouts  55 us
    unnamed x6, other arithmetic  50.2 us
    dot_general x2, matrix products, one_block(): jnp.einsum('grqk,qgrd->kgd', probs_b, grad_blk, preferred_element_type=jn...  14.5 us
  transfers between devices with their start and end apart: 7, of which 4 were waited for; matrix products, arithmetic and copies ran while one was open for 23% of the time, Pallas kernels for 0%

commit v1 on v0

--- a/solution.py
+++ b/solution.py
@@ -113,7 +113,10 @@
     trust_ratio = jnp.sqrt(weight_total) / jnp.sqrt(update_total)
     lamb_update = trust_ratio * direction
     new_local = (master_weight - learn_rate * lamb_update).astype(jnp.bfloat16)
-    new_weights = lax.all_gather(new_local, "dp", axis=0, tiled=True)
+    size = lax.axis_size("dp")
+    parts = jnp.stack([new_local for _ in range(size)])
+    parts = lax.all_to_all(parts, "dp", split_axis=0, concat_axis=0)
+    new_weights = jnp.concatenate(parts, axis=0)
     return (first_new, second_new, lamb_update, new_weights)
 
 

time: 626 us -> 684 us (1.093)
  waiting for transfers between devices: 321 us -> 368 us
  starting transfers between devices: 18.1 us -> 26.8 us
    all_to_all x0 -> x1, waiting for transfers between devices: none -> 136 us  [body(): parts = lax.all_to_all(parts, 'dp', split_axis=0, concat_axis=0)]
    all_gather x1 -> x0, waiting for transfers between devices: 89.2 us -> none  [body(): new_weights = lax.all_gather(new_local, 'dp', axis=0, tiled=True)]
    all_to_all x0 -> x1, starting transfers between devices: none -> 8.69 us  [body(): parts = lax.all_to_all(parts, 'dp', split_axis=0, concat_axis=0)]
    unnamed x4 -> x3, waiting for transfers between devices: 223 us -> 224 us
  transfers between devices with their start and end apart: 7 -> 7, of which waited for: 4 -> 4; matrix products, arithmetic and copies ran while one was open for 23% -> 21% of each run, Pallas kernels for 0% -> 0%
where the time goes in v1:
time: 684 us; the launch traced here: 680 us
  waiting for transfers between devices  368 us (54%)
  local copies, waits for them, and re-layouts  83.9 us (12%)
  blocking collectives  74.2 us (11%)
  other arithmetic  58.9 us (9%)
  matrix products  52.3 us (8%)
  starting transfers between devices  26.8 us (4%)
  between operations  15.7 us (2%)
    unnamed x3, waiting for transfers between devices  224 us
    all_to_all x1, waiting for transfers between devices, body(): parts = lax.all_to_all(parts, 'dp', split_axis=0, concat_axis=0)  136 us
    psum x1, blocking collectives, body(): weight_total, update_total = lax.psum((weight_sq, update_sq), ('dp', 'ctx'))  74.2 us
    unnamed x35, local copies, waits for them, and re-layouts  52.3 us
    unnamed x6, other arithmetic  50.2 us
    dot_general x2, matrix products, one_block(): jnp.einsum('grqk,qgrd->kgd', probs_b, grad_blk, preferred_element_type=jn...  14.5 us
  transfers between devices with their start and end apart: 7, of which 4 were waited for; matrix products, arithmetic and copies ran while one was open for 21% of the time, Pallas kernels for 0%

profile of v1, /device:TPU:36, one launch (start us, length us, event | category | flops | bytes accessed | tf_op | source)
XLA Modules:
  0.0 680.1 jit_solution(7198667600995544776)
XLA Ops:
  11.9 4.5 all-to-all-start.3
  23.9 4.1 all-to-all-start.1
  28.0 5.0 copy.102
  33.0 22.4 %reduce.3 = bf16[4096,128]{1,0:T(8,128)(2,1)S(1)} reduce(bf16[4096,1,128]{2,1,0:T(2,128)(2,1)S(1)} %bitcast.221, bf16[]{:T(256)} %broadcast.72), dimensions={1}, to_apply=%bitcast.151.reduce_sub_computation | reduce | bytes 2097154
  56.6 4.7 all-to-all-start
  61.2 5.0 copy.106
  66.3 23.4 %reduce.5 = bf16[4096,128]{1,0:T(8,128)(2,1)} reduce(bf16[4096,1,128]{2,1,0:T(2,128)(2,1)S(1)} %bitcast.220, bf16[]{:T(256)} %broadcast.72), dimensions={1}, to_apply=%bitcast.155.reduce_sub_computation | reduce | bytes 2097154
  91.9 4.8 all-to-all-start.2
  100.3 4.3 reshape.114
  107.5 5.3 all-to-all-done.2
  112.8 5.9 reshape.118
  123.9 66.5 %while.15 = (s32[]{:T(128)}, f32[1024,1,128]{0,2,1:T(8,128)S(1)}, f32[1024,1,128]{0,2,1:T(8,128)}, bf16[2,512,1,4,128]{4,3,1,0,2:T(4,128)(2,1)}, bf16[2,512,1,4,...) while((s32[]{:T(128)}, f32[1024,1,128]{0,2,1:T(8,128)S(1)}, ...), condition=%wide.region_4.5_spmd.clone, body=%wide.region_0.4_spmd.clone.sunk | while | flops 3273910784 | bytes 178353008 | solution.py:67
  134.9 5.3 fusion.84
  141.1 3.5 fusion.85
  149.2 7.3 %fusion.87 = f32[1024,1,128]{0,2,1:T(8,128)} fusion(bf16[1,512,1,4,128]{4,3,1,0,2:T(4,128)(2,1)S(1)} %get-tuple-element.238, f32[1024,1,128]{0,2,1:T(8,128)} %get-tuple-element.255, pred[]{:T(512)S(6)} %compare.3, f32[4,512]{1,0:T(4,128)S(1)} %fusion.83, f32[4,512]{1,0:T(4,128)S(1)} %get-tuple-element.241, f32[512,4,1024]{2,0,1:T(8,128)} %copy-done, ...), kind=kOutput, calls=%fused_computation.23.clone.1 | convolution fusion | flops 547618816 | bytes 10502145 | tf_op jit(solution)/shard_map/while/body/eval_jaxpr/grqk,qgrd->kgd/dot_general | solution.py:60
  168.3 5.3 fusion.84
  182.3 7.3 %fusion.87 = f32[1024,1,128]{0,2,1:T(8,128)} fusion(bf16[1,512,1,4,128]{4,3,1,0,2:T(4,128)(2,1)S(1)} %get-tuple-element.238, f32[1024,1,128]{0,2,1:T(8,128)} %get-tuple-element.255, pred[]{:T(512)S(6)} %compare.3, f32[4,512]{1,0:T(4,128)S(1)} %fusion.83, f32[4,512]{1,0:T(4,128)S(1)} %get-tuple-element.241, f32[512,4,1024]{2,0,1:T(8,128)} %copy-done, ...), kind=kOutput, calls=%fused_computation.23.clone.1 | convolution fusion | flops 547618816 | bytes 10502145 | tf_op jit(solution)/shard_map/while/body/eval_jaxpr/grqk,qgrd->kgd/dot_general | solution.py:60
  193.5 12.3 %fusion.45 = bf16[4096,768]{0,1:T(8,128)(2,1)} fusion(bf16[1,1024,4096]{2,1,0:T(8,128)(2,1)} %all-gather.2.cloned.1.call-done, bf16[1024,1,128]{2,0,1:T(8,128)(2,1)S(1)} %copy.115, bf16[1024,1,128]{2,0,1:T(8,128)(2,1)S(1)} %multiply_convert_fusion, bf16[1024,1,512]{2,0,1:T(8,128)(2,1)S(1)} %reshape.95), kind=kOutput, calls=%fused_computation.42 | convolution fusion | flops 6450315264 | bytes 16252928 | tf_op jit(solution)/shard_map/dot_general | solution.py:94
  205.8 8.8 %copy.129 = bf16[4096,768]{1,0:T(8,128)(2,1)} copy(bf16[4096,768]{0,1:T(8,128)(2,1)} %fusion.45) | data formatting | bytes 12582912
  215.8 222.9 %reduce-scatter.4.cloned.1.call-done = bf16[128,768]{1,0:T(8,128)(2,1)} async-done(((bf16[4096,768]{1,0:T(8,128)(2,1)}), bf16[128,768]{1,0:T(8,128)(2,1)}) %reduce-scatter.4.cloned.1.call-update) | async-done | bytes 196624
  440.8 74.2 %all-reduce = (f32[]{:T(128)}, f32[]{:T(128)}) all-reduce(f32[]{:T(128)} %multiply_reduce_fusion.1, f32[]{:T(128)} %get-tuple-element.171), channel_id=1, replica_groups=mesh['dp'=32,'ctx'=8] {'dp','ctx'}, use_global_device_ids=true, to_apply=%region_7.8 | all-reduce | flops 2 | bytes 16 | tf_op jit(solution)/shard_map/psum | solution.py:112
  520.0 8.7 %all-to-all-start.4 = ((bf16[32,128,768]{2,1,0:T(8,128)(2,1)}), bf16[32,128,768]{2,1,0:T(8,128)(2,1)}, u32[]{:S(2)}, u32[]{:S(2)}) async-start(bf16[32,128,768]{2,1,0:T(8,128)(2,1)} %stack.2), calls=%async_computation.4 | async-start | bytes 12582912 | tf_op jit(solution)/shard_map/all_to_all | solution.py:118
  531.4 135.9 %all-to-all-done.4 = bf16[32,128,768]{2,1,0:T(8,128)(2,1)} async-done(((bf16[32,128,768]{2,1,0:T(8,128)(2,1)}), bf16[32,128,768]{2,1,0:T(8,128)(2,1)}, u32[]{:S(2)}, u32[]{:S(2)}) %all-to-all-start.4) | async-done | bytes 6291488 | tf_op jit(solution)/shard_map/all_to_all | solution.py:118
  667.4 5.9 copy.179
  (107 shorter events, 77.5 us)
Async XLA Ops:
  11.9 12.0 %all-to-all-start.3 = ((bf16[8,2,8192]{2,1,0:T(2,128)(2,1)}), bf16[8,2,8192]{2,1,0:T(2,128)(2,1)S(1)}, u32[]{:S(2)}, u32[]{:S(2)}) async-start(bf16[8,2,8192]{2,1,0:T(2,128)(2,1)} %reshape.119), calls=%async_computation.3 | async-start | bytes 524288 | tf_op jit(solution)/shard_map/all_to_all | solution.py:90
  23.9 32.6 %all-to-all-start.1 = ((bf16[8,2,8192]{2,1,0:T(2,128)(2,1)}), bf16[8,2,8192]{2,1,0:T(2,128)(2,1)}, u32[]{:S(2)}, u32[]{:S(2)}) async-start(bf16[8,2,8192]{2,1,0:T(2,128)(2,1)} %reshape.115), calls=%async_computation.1 | async-start | bytes 524288 | tf_op jit(solution)/shard_map/all_to_all | solution.py:89
  56.6 35.3 %all-to-all-start = ((bf16[8,2,32768]{2,1,0:T(2,128)(2,1)}), bf16[8,2,32768]{2,1,0:T(2,128)(2,1)S(1)}, u32[]{:S(2)}, u32[]{:S(2)}) async-start(bf16[8,2,32768]{2,1,0:T(2,128)(2,1)} %reshape.113), calls=%async_computation | async-start | bytes 2097152 | tf_op jit(solution)/shard_map/all_to_all | solution.py:88
  91.9 8.2 %copy-start.6 = (bf16[8,2,32768]{2,1,0:T(2,128)(2,1)}, bf16[8,2,32768]{2,1,0:T(2,128)(2,1)S(1)}, u32[]{:S(2)}) copy-start(bf16[8,2,32768]{2,1,0:T(2,128)(2,1)S(1)} %all-to-all-done) | copy-start | bytes 3145732
  91.9 20.9 %all-to-all-start.2 = ((bf16[8,2,32768]{2,1,0:T(2,128)(2,1)}), bf16[8,2,32768]{2,1,0:T(2,128)(2,1)}, u32[]{:S(2)}, u32[]{:S(2)}) async-start(bf16[8,2,32768]{2,1,0:T(2,128)(2,1)} %reshape.117), calls=%async_computation.2 | async-start | bytes 2097152 | tf_op jit(solution)/shard_map/all_to_all | solution.py:91
  96.7 96.8 %all-gather.2.cloned.1.call-start = ((), (), s32[]{:S(2)}) async-start(), calls=%async_computation.6 | async-start | bytes 9437184 | tf_op jit(solution)/shard_map/all_gather | solution.py:95
  97.4 341.3 %reduce-scatter.4.cloned.1.call-start = ((), (), s32[]{:S(2)}) async-start(), calls=%async_computation.7 | async-start | bytes 6488064
  123.9 10.7 %copy-start.4 = (bf16[2,512,1,4,128]{4,3,1,0,2:T(4,128)(2,1)}, bf16[2,512,1,4,128]{4,3,1,0,2:T(4,128)(2,1)S(1)}, u32[]{:S(2)}) copy-start(bf16[2,512,1,4,128]{4,3,1,0,2:T(4,128)(2,1)S(1)} %get-tuple-element.268) | copy-start | bytes 3145732 | tf_op jit(solution)/shard_map/while
  128.9 3.2 copy-start
  134.9 6.2 copy-start.1
  134.9 6.2 copy-start.10
  144.7 2.0 copy-start.2
  149.2 7.3 %copy-start.3 = (bf16[4,512,1024]{2,1,0:T(8,128)(2,1)S(1)}, bf16[4,512,1024]{2,1,0:T(8,128)(2,1)}, u32[]{:S(2)}) copy-start(bf16[4,512,1024]{2,1,0:T(8,128)(2,1)} %copy-done.2) | copy-start | bytes 12582916 | tf_op jit(solution)/shard_map/while
  149.2 8.1 %copy-start.5 = (bf16[2,512,1,4,128]{4,3,1,0,2:T(4,128)(2,1)S(1)}, bf16[2,512,1,4,128]{4,3,1,0,2:T(4,128)(2,1)}, u32[]{:S(2)}) copy-start(bf16[2,512,1,4,128]{4,3,1,0,2:T(4,128)(2,1)} %copy-done.4) | copy-start | bytes 3145732 | tf_op jit(solution)/shard_map/while
  157.3 10.7 %copy-start.4 = (bf16[2,512,1,4,128]{4,3,1,0,2:T(4,128)(2,1)}, bf16[2,512,1,4,128]{4,3,1,0,2:T(4,128)(2,1)S(1)}, u32[]{:S(2)}) copy-start(bf16[2,512,1,4,128]{4,3,1,0,2:T(4,128)(2,1)S(1)} %get-tuple-element.268) | copy-start | bytes 3145732 | tf_op jit(solution)/shard_map/while
  162.3 3.2 copy-start
  168.3 5.9 copy-start.1
  168.3 5.9 copy-start.10
  182.3 7.3 %copy-start.3 = (bf16[4,512,1024]{2,1,0:T(8,128)(2,1)S(1)}, bf16[4,512,1024]{2,1,0:T(8,128)(2,1)}, u32[]{:S(2)}) copy-start(bf16[4,512,1024]{2,1,0:T(8,128)(2,1)} %copy-done.2) | copy-start | bytes 12582916 | tf_op jit(solution)/shard_map/while
  182.3 8.1 %copy-start.5 = (bf16[2,512,1,4,128]{4,3,1,0,2:T(4,128)(2,1)S(1)}, bf16[2,512,1,4,128]{4,3,1,0,2:T(4,128)(2,1)}, u32[]{:S(2)}) copy-start(bf16[2,512,1,4,128]{4,3,1,0,2:T(4,128)(2,1)} %copy-done.4) | copy-start | bytes 3145732 | tf_op jit(solution)/shard_map/while
  205.8 8.8 %copy-start.7 = (f32[128,768]{1,0:T(8,128)S(1)}, f32[128,768]{1,0:T(8,128)}, u32[]{:S(2)}) copy-start(f32[128,768]{1,0:T(8,128)} %param.15) | copy-start | bytes 1179652
  205.8 9.0 %copy-start.8 = (f32[128,768]{1,0:T(8,128)S(1)}, f32[128,768]{1,0:T(8,128)}, u32[]{:S(2)}) copy-start(f32[128,768]{1,0:T(8,128)} %param.16) | copy-start | bytes 1179652
  205.8 9.1 %copy-start.9 = (f32[128,768]{1,0:T(8,128)S(1)}, f32[128,768]{1,0:T(8,128)}, u32[]{:S(2)}) copy-start(f32[128,768]{1,0:T(8,128)} %param.17) | copy-start | bytes 1179652
  520.0 147.4 %all-to-all-start.4 = ((bf16[32,128,768]{2,1,0:T(8,128)(2,1)}), bf16[32,128,768]{2,1,0:T(8,128)(2,1)}, u32[]{:S(2)}, u32[]{:S(2)}) async-start(bf16[32,128,768]{2,1,0:T(8,128)(2,1)} %stack.2), calls=%async_computation.4 | async-start | bytes 12582912 | tf_op jit(solution)/shard_map/all_to_all | solution.py:118
  (1 other events, 2.0 us)
Sparse Core Ops, SparseCore 0:
  99.4 55.1 all-gather.1
  214.7 223.9 reduce-scatter.3
